TPU v7x, 256 devices: a whole 4x4x8 slice. The times are simulated.
256 devices in a mesh: claim: 64 (over y_hi, x, z), feat: 4 (over y_lo, core).
Axes of the slice: x: 4, y: 4 (y_hi: 2, y_lo: 2; y = y_hi * 2 + y_lo), z: 8, core: 2. Of those that a mesh axis runs over, the one named last changes fastest.
Arguments:
- block_tiles: bfloat16 [64, 4, 128, 128, 128], P('claim', 'feat'), may hold values from 0.049804688 to 1
- block_scale: float32 [64, 4, 128], P('claim', 'feat'), may hold values from 1 to 12, as said below
- row_index: int32 [64, 4, 128], P('claim', 'feat'), may hold values from 0 to 63
- col_index: int32 [64, 4, 128], P('claim', 'feat'), may hold values from 0 to 31
- start_basis: float32 [16384, 64], P('feat'), may hold values from -6 to 6
Outputs:
- claim_basis: float32 [524288, 64], P(('claim', 'feat'))
- feature_basis: float32 [16384, 64], P(('feat', 'claim'))
- bidiagonal: float32 [4, 64, 64], replicated
Inputs may be any that keep to these rules, and one draw needn't show every extreme that they name: `row_index`: row block within the device's 64 row blocks of claims; a few row blocks hold most stored blocks. `col_index`: column block within the device's 32 column blocks. `block_scale`: positive block scales.
All inputs are finite; a program needn't handle non-finite values.
Results may differ from a plain program's by a relative error of at most 0.012.
Values may be sent and summed in bfloat16 or wider, within the bound.
A program may use at most 64 MiB of HBM per device.

v0:
```python
import jax
import jax.numpy as jnp
from jax import lax
from jax.sharding import PartitionSpec as P

BLK_ROWS = 64
HIGH = lax.Precision.HIGHEST


def forward_local(block_tiles, block_scale, row_index, col_index, operand):
    edge = block_tiles.shape[-1]
    width = operand.shape[-1]
    picked = operand.reshape(-1, edge, width)[col_index]
    products = jnp.einsum("bij,bjk->bik", block_tiles, picked, preferred_element_type=jnp.float32)
    products = products * block_scale[:, None, None]
    selector = (row_index[None, :] == jnp.arange(BLK_ROWS, dtype=jnp.int32)[:, None]).astype(
        jnp.float32
    )
    summed = jnp.einsum("rb,bik->rik", selector, products, precision=HIGH)
    return summed.reshape(BLK_ROWS * edge, width)


def backward_local(block_tiles, block_scale, row_index, col_index, operand, col_count):
    edge = block_tiles.shape[-1]
    width = operand.shape[-1]
    picked = operand.reshape(-1, edge, width)[row_index]
    products = jnp.einsum("bij,bik->bjk", block_tiles, picked, preferred_element_type=jnp.float32)
    products = products * block_scale[:, None, None]
    selector = (col_index[None, :] == jnp.arange(col_count, dtype=jnp.int32)[:, None]).astype(
        jnp.float32
    )
    summed = jnp.einsum("cb,bjk->cjk", selector, products, precision=HIGH)
    return summed.reshape(col_count * edge, width)


def degree_local(block_tiles, block_scale, row_index, col_index, col_count):
    row_sums = jnp.sum(block_tiles, axis=2, dtype=jnp.float32) * block_scale[:, None]
    col_sums = jnp.sum(block_tiles, axis=1, dtype=jnp.float32) * block_scale[:, None]
    row_select = (row_index[None, :] == jnp.arange(BLK_ROWS, dtype=jnp.int32)[:, None]).astype(
        jnp.float32
    )
    col_select = (col_index[None, :] == jnp.arange(col_count, dtype=jnp.int32)[:, None]).astype(
        jnp.float32
    )
    row_part = jnp.einsum("rb,bi->ri", row_select, row_sums, precision=HIGH).reshape(-1)
    col_part = jnp.einsum("cb,bi->ci", col_select, col_sums, precision=HIGH).reshape(-1)
    return (row_part, col_part)


def gram_of(block):
    return jnp.dot(block.T, block, precision=HIGH)


def orthonormal(block, gram_total):
    factor = jnp.linalg.cholesky(gram_total)
    basis = lax.linalg.triangular_solve(
        factor, block, left_side=False, lower=True, transpose_a=True
    )
    return (basis, factor.T)


def per_device(block_tiles, block_scale, row_index, col_index, start_basis):
    tiles_here = block_tiles.reshape(block_tiles.shape[2:])
    scale_here = block_scale.reshape(-1)
    rows_here = row_index.reshape(-1)
    cols_here = col_index.reshape(-1)
    edge = tiles_here.shape[-1]
    col_count = start_basis.shape[0] // edge
    claim_count = lax.axis_size("claim")
    own_cols = start_basis.shape[0] // claim_count
    own_first = lax.axis_index("claim") * own_cols
    row_part, col_part = degree_local(tiles_here, scale_here, rows_here, cols_here, col_count)
    col_total = lax.psum(col_part, "claim")
    col_scale = lax.rsqrt(col_total + 1.0)
    row_total = lax.psum_scatter(row_part, "feat", scatter_dimension=0, tiled=True)
    start_total = lax.psum(gram_of(start_basis), "feat")
    first_basis, _ = orthonormal(start_basis, start_total)
    first_operand = (col_scale[:, None] * first_basis).astype(jnp.bfloat16)
    first_partial = forward_local(tiles_here, scale_here, rows_here, cols_here, first_operand)
    first_sums = lax.psum_scatter(first_partial, "feat", scatter_dimension=0, tiled=True)
    row_scale = lax.rsqrt(row_total + 1.0)

    def row_orthonormal(block):
        total = lax.psum(gram_of(block), ("claim", "feat"))
        return orthonormal(block, total)

    def backward_partial(basis):
        operand = (row_scale[:, None] * basis).astype(jnp.bfloat16)
        gathered = lax.all_gather(operand, "feat", axis=0, tiled=True)
        return backward_local(tiles_here, scale_here, rows_here, cols_here, gathered, col_count)

    def column_update(partial_value, previous, coupling):
        summed = lax.psum(partial_value, "claim")
        update = col_scale[:, None] * summed - jnp.dot(previous, coupling.T, precision=HIGH)
        total = lax.psum(gram_of(update), "feat")
        return orthonormal(update, total)

    u_first, b_first = row_orthonormal(row_scale[:, None] * first_sums)
    v_second, a_second = column_update(backward_partial(u_first), first_basis, b_first)
    scaled = (col_scale[:, None] * v_second).astype(jnp.bfloat16)
    second_partial = forward_local(tiles_here, scale_here, rows_here, cols_here, scaled)
    second_sums = lax.psum_scatter(second_partial, "feat", scatter_dimension=0, tiled=True)
    p_second = row_scale[:, None] * second_sums - jnp.dot(u_first, a_second.T, precision=HIGH)
    u_second, b_second = row_orthonormal(p_second)
    v_third, a_third = column_update(backward_partial(u_second), v_second, b_second)
    v_output = lax.dynamic_slice_in_dim(v_third, own_first, own_cols, 0)
    bidiagonal = jnp.stack([b_first, a_second, b_second, a_third])
    return (u_second, v_output, bidiagonal)


def solution(mesh):
    placed = (
        P("claim", "feat", None, None, None),
        P("claim", "feat", None),
        P("claim", "feat", None),
        P("claim", "feat", None),
        P("feat", None),
    )
    return jax.shard_map(
        per_device,
        mesh=mesh,
        in_specs=placed,
        out_specs=(P(("claim", "feat"), None), P(("feat", "claim"), None), P()),
        check_vma=False,
    )
```

profile of v0, /device:TPU:1, one launch (start us, length us, event | category | flops | bytes accessed | tf_op | source)
XLA Modules:
  0.0 2190.3 jit_solution(12832989908346976326)
XLA Ops:
  7.3 1.1 copy-done
  8.4 1.0 fusion.96
  9.4 3.4 convert_reduce_fusion.1
  13.1 13.1 all-reduce.1
  26.3 5.8 cholesky.89
  32.2 0.6 compare_reduce_fusion.4
  32.8 0.7 fusion.33
  33.5 4.9 custom-call.11
  38.4 1.0 convolution_bitcast_fusion.2
  39.6 305.2 %psum.56 = f32[4096]{0:T(1024)S(1)} all-reduce(f32[4096]{0:T(1024)S(1)} %convolution_bitcast_fusion.6), channel_id=1, replica_groups=mesh['claim'=64,'feat'=4] {'claim'}, use_global_device_ids=true, to_apply=%region_3.0 | all-reduce | flops 4096 | bytes 32768 | tf_op jit(solution)/shard_map/psum | solution.py:73
  345.0 2.2 gather_fusion
  347.1 5.8 multiply_bitcast_fusion.3
  352.9 4.2 fusion.14
  357.1 2.5 copy.86
  361.0 77.3 %reduce-scatter.3.cloned.1.call-done = f32[2048,64]{0,1:T(8,128)} async-done(((f32[8192,64]{0,1:T(8,128)}), f32[2048,64]{0,1:T(8,128)}) %reduce-scatter.3.cloned.1.call-update) | async-done | bytes 524304 | tf_op jit(solution)/shard_map/reduce_scatter | solution.py:80
  438.3 1.8 fusion.27
  440.1 77.1 %psum.58 = f32[64,64]{0,1:T(8,128)S(1)} all-reduce(f32[64,64]{0,1:T(8,128)S(1)} %fusion.27), channel_id=1, replica_groups=mesh['claim'=64,'feat'=4] {'claim','feat'}, use_global_device_ids=true, to_apply=%region_8.11 | all-reduce | flops 4096 | bytes 32768 | tf_op jit(solution)/shard_map/psum | solution.py:84
  517.4 5.8 cholesky.100
  523.9 0.7 fusion.67
  524.5 4.9 custom-call.12
  529.4 2.6 multiply_convert_fusion.3
  532.3 19.8 all-gather.3.cloned.1.call-done
  552.1 1.5 copy_bitcast_fusion.5
  553.6 2.2 gather_fusion.1
  555.8 4.0 multiply_bitcast_fusion.2
  559.8 3.9 fusion.12
  563.8 1.6 copy.88
  565.5 648.9 %all-reduce.5.cloned.1.call-done = f32[4096,64]{0,1:T(8,128)} async-done(((f32[4096,64]{0,1:T(8,128)}), f32[4096,64]{0,1:T(8,128)}) %all-reduce.5.cloned.1.call-update) | async-done | bytes 1048592 | tf_op jit(solution)/shard_map/psum | solution.py:93
  1214.4 2.9 convolution_subtract_fusion.1
  1217.3 1.0 fusion.97
  1218.3 56.8 %psum.60 = f32[64,64]{0,1:T(8,128)S(1)} all-reduce(f32[64,64]{0,1:T(8,128)S(1)} %fusion.97), channel_id=1, replica_groups=mesh['claim'=64,'feat'=4] {'feat'}, use_global_device_ids=true, to_apply=%region_10.14 | all-reduce | flops 4096 | bytes 32768 | tf_op jit(solution)/shard_map/psum | solution.py:95
  1275.2 5.8 cholesky.111
  1281.1 0.6 compare_reduce_fusion.2
  1281.7 0.7 fusion.65
  1282.4 4.9 custom-call.13
  1287.3 1.1 convolution_bitcast_fusion.1
  1288.5 2.2 gather_fusion.2
  1290.7 5.8 multiply_bitcast_fusion.1
  1296.5 4.2 fusion.10
  1300.6 2.5 copy.85
  1303.2 28.4 %reduce-scatter.5.cloned.1.call-done = f32[2048,64]{0,1:T(8,128)} async-done(((f32[8192,64]{0,1:T(8,128)}), f32[2048,64]{0,1:T(8,128)}) %reduce-scatter.5.cloned.1.call-update) | async-done | bytes 524304 | tf_op jit(solution)/shard_map/reduce_scatter | solution.py:102
  1331.6 2.3 convolution_subtract_fusion.2
  1334.5 77.3 %psum.61 = f32[64,64]{0,1:T(8,128)S(1)} all-reduce(f32[64,64]{0,1:T(8,128)S(1)} %fusion.98), channel_id=1, replica_groups=mesh['claim'=64,'feat'=4] {'claim','feat'}, use_global_device_ids=true, to_apply=%region_12.16 | all-reduce | flops 4096 | bytes 32768 | tf_op jit(solution)/shard_map/psum | solution.py:84
  1411.9 5.8 cholesky.122
  1418.4 0.7 fusion.63
  1419.1 4.9 custom-call.14
  1424.0 1.5 multiply_convert_fusion.2
  1425.6 20.0 all-gather.5.cloned.1.call-done
  1445.6 1.5 copy_bitcast_fusion.4
  1447.2 2.2 gather_fusion.3
  1449.3 4.0 multiply_bitcast_fusion
  1453.4 3.9 fusion.8
  1457.3 1.6 copy.87
  1459.0 648.9 %all-reduce.7.cloned.1.call-done = f32[4096,64]{0,1:T(8,128)} async-done(((f32[4096,64]{0,1:T(8,128)}), f32[4096,64]{0,1:T(8,128)}) %all-reduce.7.cloned.1.call-update) | async-done | bytes 1048592 | tf_op jit(solution)/shard_map/psum | solution.py:93
  2107.9 2.9 convolution_subtract_fusion
  2110.8 1.0 fusion.99
  2111.8 56.6 %psum.63 = f32[64,64]{0,1:T(8,128)S(1)} all-reduce(f32[64,64]{0,1:T(8,128)S(1)} %fusion.99), channel_id=1, replica_groups=mesh['claim'=64,'feat'=4] {'feat'}, use_global_device_ids=true, to_apply=%region_14.18 | all-reduce | flops 4096 | bytes 32768 | tf_op jit(solution)/shard_map/psum | solution.py:95
  2168.5 5.8 cholesky.133
  2174.4 0.6 compare_reduce_fusion
  2175.0 0.7 fusion.62
  2175.7 4.9 custom-call.15
  2180.6 1.0 convolution_bitcast_fusion
  2181.7 0.7 copy.54
  2182.4 0.8 copy.55
  (54 shorter events, 4.4 us)
Async XLA Ops:
  7.2 1.2 copy-start
  7.2 5.6 copy-start.2
  7.2 5.6 copy-start.3
  7.2 32.2 %copy-start.4 = (s32[1,1,128]{2,1,0:T(1,128)S(1)}, s32[1,1,128]{2,1,0:T(1,128)}, u32[]{:S(2)}) copy-start(s32[1,1,128]{2,1,0:T(1,128)} %param.13) | copy-start | bytes 1540
  7.2 431.1 %reduce-scatter.3.cloned.1.call-start = ((), (), s32[]{:S(2)}) async-start(), calls=%async_computation.2 | async-start | bytes 2621440 | tf_op jit(solution)/shard_map/reduce_scatter | solution.py:80
  357.1 2.6 copy-start.5
  359.7 192.4 %all-gather.3.cloned.1.call-start = ((), (), s32[]{:S(2)}) async-start(), calls=%async_computation.3 | async-start | bytes 1310720 | tf_op jit(solution)/shard_map/all_gather | solution.py:89
  532.0 682.4 %all-reduce.5.cloned.1.call-start = ((), (), s32[]{:S(2)}) async-start(), calls=%async_computation.4 | async-start | bytes 2097152 | tf_op jit(solution)/shard_map/psum | solution.py:93
  565.4 766.2 %reduce-scatter.5.cloned.1.call-start = ((), (), s32[]{:S(2)}) async-start(), calls=%async_computation.5 | async-start | bytes 2621440 | tf_op jit(solution)/shard_map/reduce_scatter | solution.py:102
  1300.6 31.0 %copy-start.1 = (f32[2048,64]{0,1:T(8,128)S(1)}, f32[2048,64]{0,1:T(8,128)}, u32[]{:S(2)}) copy-start(f32[2048,64]{0,1:T(8,128)} %get-tuple-element.28) | copy-start | bytes 1572868
  1303.2 142.4 %all-gather.5.cloned.1.call-start = ((), (), s32[]{:S(2)}) async-start(), calls=%async_computation.6 | async-start | bytes 1310720 | tf_op jit(solution)/shard_map/all_gather | solution.py:89
  1425.6 682.3 %all-reduce.7.cloned.1.call-start = ((), (), s32[]{:S(2)}) async-start(), calls=%async_computation.7 | async-start | bytes 2097152 | tf_op jit(solution)/shard_map/psum | solution.py:93
Sparse Core Ops, SparseCore 0:
  359.8 78.4 reduce-scatter.2
  532.2 19.9 all-gather.2
  565.6 648.7 all-reduce.4
  1303.3 28.2 reduce-scatter.4
  1425.7 19.9 all-gather.4
  1459.1 648.7 all-reduce.6
where the time goes:
time: 2200 us; the launch traced here: 2190 us
  waiting for transfers between devices  1440 us (65%)
  blocking collectives  586 us (27%)
  other arithmetic  64.1 us (3%)
  matrix products  57 us (3%)
  local copies, waits for them, and re-layouts  23.7 us (1%)
    psum x2, waiting for transfers between devices, column_update(): summed = lax.psum(partial_value, 'claim')  1300 us
    psum x1, blocking collectives, per_device(): col_total = lax.psum(col_part, 'claim')  305 us
    psum x2, blocking collectives, row_orthonormal(): total = lax.psum(gram_of(block), ('claim', 'feat'))  154 us
    psum x2, blocking collectives, column_update(): total = lax.psum(gram_of(update), 'feat')  113 us
    reduce_scatter x1, waiting for transfers between devices, per_device(): lax.psum_scatter(first_partial, 'feat', scatter_dimension=0, tiled=True)  77.3 us
  transfers between devices with their start and end apart: 6, of which 6 were waited for; matrix products, arithmetic and copies ran while one was open for 0% of the time, Pallas kernels for 0%

commit v1 on v0

--- a/solution.py
+++ b/solution.py
@@ -81,7 +81,7 @@
     row_scale = lax.rsqrt(row_total + 1.0)
 
     def row_orthonormal(block):
-        total = lax.psum(gram_of(block), ("claim", "feat"))
+        total = lax.psum(lax.psum(gram_of(block), "claim"), "feat")
         return orthonormal(block, total)
 
     def backward_partial(basis):

time: 2200 us -> 2770 us (1.26)
  blocking collectives: 586 us -> 1170 us
    psum x2 -> x4, blocking collectives: 154 us -> 737 us  [row_orthonormal(): total = lax.psum(lax.psum(gram_of(block), 'claim'), 'feat')]
where the time goes in v1:
time: 2770 us; the launch traced here: 2760 us
  waiting for transfers between devices  1430 us (52%)
  blocking collectives  1170 us (42%)
  other arithmetic  64.1 us (2%)
  matrix products  57 us (2%)
    psum x2, waiting for transfers between devices, column_update(): summed = lax.psum(partial_value, 'claim')  1300 us
    psum x4, blocking collectives, row_orthonormal(): total = lax.psum(lax.psum(gram_of(block), 'claim'), 'feat')  737 us
    psum x1, blocking collectives, per_device(): col_total = lax.psum(col_part, 'claim')  305 us
    psum x2, blocking collectives, column_update(): total = lax.psum(gram_of(update), 'feat')  113 us
    reduce_scatter x1, waiting for transfers between devices, per_device(): lax.psum_scatter(first_partial, 'feat', scatter_dimension=0, tiled=True)  77.3 us
  transfers between devices with their start and end apart: 6, of which 6 were waited for; matrix products, arithmetic and copies ran while one was open for 0% of the time, Pallas kernels for 0%

profile of v1, /device:TPU:1, one launch (start us, length us, event | category | flops | bytes accessed | tf_op | source)
XLA Modules:
  0.0 2763.5 jit_solution(7869802394764516723)
XLA Ops:
  7.3 1.1 copy-done
  8.4 1.0 fusion.96
  9.4 3.4 convert_reduce_fusion.1
  13.1 13.1 all-reduce.1
  26.3 5.8 cholesky.89
  32.2 0.6 compare_reduce_fusion.4
  32.8 0.7 fusion.33
  33.5 4.9 custom-call.11
  38.4 1.0 convolution_bitcast_fusion.2
  39.6 305.2 %psum.70 = f32[4096]{0:T(1024)S(1)} all-reduce(f32[4096]{0:T(1024)S(1)} %convolution_bitcast_fusion.6), channel_id=1, replica_groups=mesh['claim'=64,'feat'=4] {'claim'}, use_global_device_ids=true, to_apply=%region_3.0 | all-reduce | flops 4096 | bytes 32768 | tf_op jit(solution)/shard_map/psum | solution.py:73
  345.0 2.2 gather_fusion
  347.1 5.8 multiply_bitcast_fusion.3
  352.9 4.2 fusion.14
  357.1 2.5 copy.86
  361.0 77.3 %reduce-scatter.3.cloned.1.call-done = f32[2048,64]{0,1:T(8,128)} async-done(((f32[8192,64]{0,1:T(8,128)}), f32[2048,64]{0,1:T(8,128)}) %reduce-scatter.3.cloned.1.call-update) | async-done | bytes 524304 | tf_op jit(solution)/shard_map/reduce_scatter | solution.py:80
  438.3 1.8 fusion.27
  440.1 303.0 %psum.72 = f32[64,64]{0,1:T(8,128)S(1)} all-reduce(f32[64,64]{0,1:T(8,128)S(1)} %fusion.27), channel_id=1, replica_groups=mesh['claim'=64,'feat'=4] {'claim'}, use_global_device_ids=true, to_apply=%region_8.11 | all-reduce | flops 4096 | bytes 32768 | tf_op jit(solution)/shard_map/psum | solution.py:84
  743.1 65.3 %psum.73 = f32[64,64]{0,1:T(8,128)S(1)} all-reduce(f32[64,64]{0,1:T(8,128)S(1)} %psum.72), channel_id=1, replica_groups=mesh['claim'=64,'feat'=4] {'feat'}, use_global_device_ids=true, to_apply=%region_9.12 | all-reduce | flops 4096 | bytes 32768 | tf_op jit(solution)/shard_map/psum | solution.py:84
  808.5 5.8 cholesky.100
  815.1 0.7 fusion.67
  815.7 4.9 custom-call.12
  820.6 2.6 multiply_convert_fusion.3
  823.5 15.2 all-gather.3.cloned.1.call-done
  838.7 1.5 copy_bitcast_fusion.5
  840.2 2.2 gather_fusion.1
  842.4 4.0 multiply_bitcast_fusion.2
  846.5 3.9 fusion.12
  850.4 1.6 copy.88
  852.1 648.9 %all-reduce.5.cloned.1.call-done = f32[4096,64]{0,1:T(8,128)} async-done(((f32[4096,64]{0,1:T(8,128)}), f32[4096,64]{0,1:T(8,128)}) %all-reduce.5.cloned.1.call-update) | async-done | bytes 1048592 | tf_op jit(solution)/shard_map/psum | solution.py:93
  1501.0 2.9 convolution_subtract_fusion.1
  1504.0 1.0 fusion.97
  1504.9 56.8 %psum.75 = f32[64,64]{0,1:T(8,128)S(1)} all-reduce(f32[64,64]{0,1:T(8,128)S(1)} %fusion.97), channel_id=1, replica_groups=mesh['claim'=64,'feat'=4] {'feat'}, use_global_device_ids=true, to_apply=%region_11.15 | all-reduce | flops 4096 | bytes 32768 | tf_op jit(solution)/shard_map/psum | solution.py:95
  1561.8 5.8 cholesky.111
  1568.3 0.7 fusion.65
  1569.0 4.9 custom-call.13
  1573.9 1.1 convolution_bitcast_fusion.1
  1575.1 2.2 gather_fusion.2
  1577.3 5.8 multiply_bitcast_fusion.1
  1583.1 4.2 fusion.10
  1587.2 2.5 copy.85
  1589.9 28.4 %reduce-scatter.5.cloned.1.call-done = f32[2048,64]{0,1:T(8,128)} async-done(((f32[8192,64]{0,1:T(8,128)}), f32[2048,64]{0,1:T(8,128)}) %reduce-scatter.5.cloned.1.call-update) | async-done | bytes 524304 | tf_op jit(solution)/shard_map/reduce_scatter | solution.py:102
  1618.3 2.3 convolution_subtract_fusion.2
  1621.1 303.0 %psum.76 = f32[64,64]{0,1:T(8,128)S(1)} all-reduce(f32[64,64]{0,1:T(8,128)S(1)} %fusion.98), channel_id=1, replica_groups=mesh['claim'=64,'feat'=4] {'claim'}, use_global_device_ids=true, to_apply=%region_13.17 | all-reduce | flops 4096 | bytes 32768 | tf_op jit(solution)/shard_map/psum | solution.py:84
  1924.1 65.6 %psum.77 = f32[64,64]{0,1:T(8,128)S(1)} all-reduce(f32[64,64]{0,1:T(8,128)S(1)} %psum.76), channel_id=1, replica_groups=mesh['claim'=64,'feat'=4] {'feat'}, use_global_device_ids=true, to_apply=%region_14.18 | all-reduce | flops 4096 | bytes 32768 | tf_op jit(solution)/shard_map/psum | solution.py:84
  1989.8 5.8 cholesky.122
  1996.3 0.7 fusion.63
  1997.0 4.9 custom-call.14
  2001.9 1.5 multiply_convert_fusion.2
  2003.5 15.4 all-gather.5.cloned.1.call-done
  2018.8 1.5 copy_bitcast_fusion.4
  2020.4 2.2 gather_fusion.3
  2022.5 4.0 multiply_bitcast_fusion
  2026.6 3.9 fusion.8
  2030.5 1.6 copy.87
  2032.2 648.9 %all-reduce.7.cloned.1.call-done = f32[4096,64]{0,1:T(8,128)} async-done(((f32[4096,64]{0,1:T(8,128)}), f32[4096,64]{0,1:T(8,128)}) %all-reduce.7.cloned.1.call-update) | async-done | bytes 1048592 | tf_op jit(solution)/shard_map/psum | solution.py:93
  2681.1 2.9 convolution_subtract_fusion
  2684.0 1.0 fusion.99
  2685.0 56.6 %psum.79 = f32[64,64]{0,1:T(8,128)S(1)} all-reduce(f32[64,64]{0,1:T(8,128)S(1)} %fusion.99), channel_id=1, replica_groups=mesh['claim'=64,'feat'=4] {'feat'}, use_global_device_ids=true, to_apply=%region_16.20 | all-reduce | flops 4096 | bytes 32768 | tf_op jit(solution)/shard_map/psum | solution.py:95
  2741.7 5.8 cholesky.133
  2748.2 0.7 fusion.62
  2748.9 4.9 custom-call.15
  2753.8 1.0 convolution_bitcast_fusion
  2754.9 0.7 copy.54
  2755.7 0.8 copy.55
  (56 shorter events, 5.7 us)
Async XLA Ops:
  7.2 1.2 copy-start
  7.2 5.6 copy-start.2
  7.2 5.6 copy-start.3
  7.2 32.2 %copy-start.4 = (s32[1,1,128]{2,1,0:T(1,128)S(1)}, s32[1,1,128]{2,1,0:T(1,128)}, u32[]{:S(2)}) copy-start(s32[1,1,128]{2,1,0:T(1,128)} %param.13) | copy-start | bytes 1540
  7.2 431.1 %reduce-scatter.3.cloned.1.call-start = ((), (), s32[]{:S(2)}) async-start(), calls=%async_computation.2 | async-start | bytes 2621440 | tf_op jit(solution)/shard_map/reduce_scatter | solution.py:80
  357.1 2.6 copy-start.5
  359.7 479.0 %all-gather.3.cloned.1.call-start = ((), (), s32[]{:S(2)}) async-start(), calls=%async_computation.3 | async-start | bytes 1310720 | tf_op jit(solution)/shard_map/all_gather | solution.py:89
  823.2 677.8 %all-reduce.5.cloned.1.call-start = ((), (), s32[]{:S(2)}) async-start(), calls=%async_computation.4 | async-start | bytes 2097152 | tf_op jit(solution)/shard_map/psum | solution.py:93
  852.1 766.2 %reduce-scatter.5.cloned.1.call-start = ((), (), s32[]{:S(2)}) async-start(), calls=%async_computation.5 | async-start | bytes 2621440 | tf_op jit(solution)/shard_map/reduce_scatter | solution.py:102
  1587.2 31.0 %copy-start.1 = (f32[2048,64]{0,1:T(8,128)S(1)}, f32[2048,64]{0,1:T(8,128)}, u32[]{:S(2)}) copy-start(f32[2048,64]{0,1:T(8,128)} %get-tuple-element.28) | copy-start | bytes 1572868
  1589.8 429.0 %all-gather.5.cloned.1.call-start = ((), (), s32[]{:S(2)}) async-start(), calls=%async_computation.6 | async-start | bytes 1310720 | tf_op jit(solution)/shard_map/all_gather | solution.py:89
  2003.4 677.7 %all-reduce.7.cloned.1.call-start = ((), (), s32[]{:S(2)}) async-start(), calls=%async_computation.7 | async-start | bytes 2097152 | tf_op jit(solution)/shard_map/psum | solution.py:93
Sparse Core Ops, SparseCore 0:
  359.8 78.4 reduce-scatter.2
  823.3 15.3 all-gather.2
  852.2 648.7 all-reduce.4
  1589.9 28.2 reduce-scatter.4
  2003.6 15.2 all-gather.4
  2032.3 648.7 all-reduce.6
